TPU v7x, 32 devices: a whole 2x2x4 slice. The times are simulated.
32 devices in a mesh: seq: 8 (over z, y), head: 4 (over x, core).
Axes of the slice: x: 2, y: 2, z: 4, core: 2. Of those that a mesh axis runs over, the one named last changes fastest.
Arguments:
- hidden_states: bfloat16 [4096, 4096], P('seq', 'head'), may hold values from -64 to 64
- out_grad: bfloat16 [4096, 4096], P('seq', 'head'), may hold values from -96 to 96
- encodings: bfloat16 [4096, 896], P('seq'), may hold values from -9 to 9
- w_query: bfloat16 [4096, 2048], P(None, 'head'), may hold values from -1 to 1
- w_key: bfloat16 [896, 2048], P(None, 'head'), may hold values from -1 to 1
- w_value: bfloat16 [896, 2048], P(None, 'head'), may hold values from -0.1875 to 0.1875
- w_out: bfloat16 [2048, 4096], P('head'), may hold values from -0.125 to 0.125
- neighbour_ids: int32 [64, 2], P('seq'), may hold values from 0 to 31, as said below
- neighbour_counts: int32 [64], P('seq'), may hold values from 1 to 2
Outputs:
- hidden_grad: bfloat16 [4096, 4096], P(('seq', 'head'))
- enc_grad: bfloat16 [4096, 896], P('seq', 'head')
Inputs may be any that keep to these rules, and one draw needn't show every extreme that they name: `neighbour_ids`: record b lies in the shard of seq index b // 4. The 16 entries of the spans of one seq index name at most 2 records of any one shard, and exactly 2 of one shard that every seq index names so.
All inputs are finite; a program needn't handle non-finite values.
Results may differ from a plain program's by a relative error of at most 0.01.
The roundings to bfloat16 on the way count: a program that leaves them out, or rounds other values in their place, can miss the bound.
Values may be sent and summed in bfloat16 or wider, within the bound.
No kernel may reach another device: no remote copies, remote signals or barrier semaphores. Data moves between devices by JAX's collectives and lax.ppermute only.
A program may use at most 128 MiB of HBM per device.

v0:
```python
import math

import jax
import jax.numpy as jnp
from jax import lax
from jax.sharding import PartitionSpec as P

HD = 128
SPAN = 64
NEIGH = 2
RET = 128


def attend_spans(queries, attend_grad, key_rows, value_rows, record_counts):
    row_count = queries.shape[0]
    columns = queries.shape[1]
    heads_here = columns // HD
    spans_here = row_count // SPAN
    shift_by = SPAN - 1
    score_scale = 1.0 / math.sqrt(HD)
    has_keys = jnp.arange(row_count) < row_count - shift_by
    query_rows = jnp.roll(queries, -shift_by, axis=0).reshape(spans_here, SPAN, heads_here, HD)
    grad_rows = jnp.where(
        has_keys[:, None], jnp.roll(attend_grad, -shift_by, axis=0), jnp.zeros((), jnp.bfloat16)
    )
    grad_rows = grad_rows.reshape(spans_here, SPAN, heads_here, HD)
    key_spans = key_rows.reshape(spans_here, NEIGH * RET, heads_here, HD)
    value_spans = value_rows.reshape(spans_here, NEIGH * RET, heads_here, HD)
    in_use = jnp.arange(NEIGH)[None, :] < record_counts[:, None]
    key_in_use = jnp.repeat(in_use, RET, axis=1)
    scores = (
        jnp.einsum("cqhd,ckhd->chqk", query_rows, key_spans, preferred_element_type=jnp.float32)
        * score_scale
    )
    scores = jnp.where(key_in_use[:, None, None, :], scores, -jnp.inf)
    row_top = jnp.max(scores, axis=-1, keepdims=True)
    exponent = jnp.exp(scores - row_top)
    soft_weights = exponent / jnp.sum(exponent, axis=-1, keepdims=True)
    soft_low = soft_weights.astype(jnp.bfloat16)
    outputs = jnp.einsum(
        "chqk,ckhd->cqhd", soft_low, value_spans, preferred_element_type=jnp.float32
    )
    row_delta = jnp.sum(grad_rows.astype(jnp.float32) * outputs, axis=-1)
    prob_grad = jnp.einsum(
        "cqhd,ckhd->chqk", grad_rows, value_spans, preferred_element_type=jnp.float32
    )
    score_grad = soft_weights * (prob_grad - jnp.transpose(row_delta, (0, 2, 1))[..., None])
    score_low = score_grad.astype(jnp.bfloat16)
    query_grad = (
        jnp.einsum("chqk,ckhd->cqhd", score_low, key_spans, preferred_element_type=jnp.float32)
        * score_scale
    ).astype(jnp.bfloat16)
    key_grad = (
        jnp.einsum("chqk,cqhd->ckhd", score_low, query_rows, preferred_element_type=jnp.float32)
        * score_scale
    ).astype(jnp.bfloat16)
    value_grad = jnp.einsum(
        "chqk,cqhd->ckhd", soft_low, grad_rows, preferred_element_type=jnp.float32
    ).astype(jnp.bfloat16)
    query_grad = jnp.roll(query_grad.reshape(row_count, columns), shift_by, axis=0)
    pair_total = spans_here * NEIGH
    return (
        query_grad,
        key_grad.reshape(pair_total, RET, columns),
        value_grad.reshape(pair_total, RET, columns),
    )


def shards(
    hidden_states,
    out_grad,
    encodings,
    w_query,
    w_key,
    w_value,
    w_out,
    neighbour_ids,
    neighbour_counts,
):
    seq_count = lax.axis_size("seq")
    columns = w_query.shape[1]
    record_total = encodings.shape[0] // RET
    requests = neighbour_ids.shape[0] * NEIGH
    slot_cap = max(2, (requests + seq_count - 1) // seq_count)
    slot_total = seq_count * slot_cap
    highest = lax.Precision.HIGHEST
    contract_last = (((1,), (1,)), ((), ()))
    contract_first = (((0,), (0,)), ((), ()))
    hidden_piece = lax.all_gather(hidden_states, "head", axis=1, tiled=True)
    grad_piece = lax.all_gather(out_grad, "head", axis=1, tiled=True)
    query_sum = jnp.dot(hidden_piece, w_query, preferred_element_type=jnp.float32)
    grad_sum = lax.dot_general(grad_piece, w_out, contract_last, preferred_element_type=jnp.float32)
    query_sum, grad_sum = (query_sum, grad_sum)
    queries = query_sum.astype(jnp.bfloat16)
    attend_grad = grad_sum.astype(jnp.bfloat16)
    wanted = neighbour_ids.reshape(requests)
    owner_of = wanted // record_total
    local_record = wanted % record_total
    order_at = jnp.arange(requests)
    earlier_same = (owner_of[:, None] == owner_of[None, :]) & (
        order_at[None, :] < order_at[:, None]
    )
    rank_at = jnp.sum(earlier_same, axis=1)
    slot_at = owner_of * slot_cap + rank_at
    placing = slot_at[:, None] == jnp.arange(slot_total)[None, :]
    placing_low = placing.astype(jnp.bfloat16)
    slot_record = jnp.sum(jnp.where(placing, local_record[:, None], 0), axis=0)
    slot_record = jnp.where(jnp.any(placing, axis=0), slot_record, -1).reshape(seq_count, slot_cap)
    asked = lax.all_to_all(slot_record, "seq", split_axis=0, concat_axis=0, tiled=True).reshape(
        slot_total
    )
    choosing = asked[:, None] == jnp.arange(record_total)[None, :]
    choosing_low = choosing.astype(jnp.bfloat16)
    key_own = jnp.dot(encodings, w_key, preferred_element_type=jnp.float32).astype(jnp.bfloat16)
    value_own = jnp.dot(encodings, w_value, preferred_element_type=jnp.float32).astype(jnp.bfloat16)
    paired_own = jnp.concatenate([key_own, value_own], axis=1).reshape(
        record_total, RET * 2 * columns
    )
    outgoing = jnp.dot(choosing_low, paired_own, preferred_element_type=jnp.float32).astype(
        jnp.bfloat16
    )
    arrived = lax.all_to_all(
        outgoing.reshape(seq_count, slot_cap, RET, 2 * columns),
        "seq",
        split_axis=0,
        concat_axis=0,
        tiled=True,
    )
    fetched = jnp.dot(
        placing_low,
        arrived.reshape(slot_total, RET * 2 * columns),
        preferred_element_type=jnp.float32,
    ).astype(jnp.bfloat16)
    fetched = fetched.reshape(requests, RET, 2 * columns)
    key_rows = fetched[:, :, :columns]
    value_rows = fetched[:, :, columns:]
    query_grad, key_grad, value_grad = attend_spans(
        queries, attend_grad, key_rows, value_rows, neighbour_counts
    )
    paired_grad = jnp.concatenate([key_grad, value_grad], axis=2).reshape(
        requests, RET * 2 * columns
    )
    returning = lax.dot_general(
        placing_low, paired_grad, contract_first, preferred_element_type=jnp.float32
    ).astype(jnp.bfloat16)
    came_back = lax.all_to_all(
        returning.reshape(seq_count, slot_cap, RET, 2 * columns),
        "seq",
        split_axis=0,
        concat_axis=0,
        tiled=True,
    )
    record_grad = lax.dot_general(
        choosing_low,
        came_back.reshape(slot_total, RET * 2 * columns),
        contract_first,
        preferred_element_type=jnp.float32,
    )
    record_grad = record_grad.reshape(record_total * RET, 2 * columns)
    enc_part = lax.dot_general(
        record_grad[:, :columns], w_key.astype(jnp.float32), contract_last, precision=highest
    )
    enc_part = enc_part + lax.dot_general(
        record_grad[:, columns:], w_value.astype(jnp.float32), contract_last, precision=highest
    )
    enc_grad = lax.psum_scatter(enc_part, "head", scatter_dimension=1, tiled=True).astype(
        jnp.bfloat16
    )
    partial_value = lax.dot_general(
        query_grad, w_query, contract_last, preferred_element_type=jnp.float32
    )
    hidden_grad = lax.psum_scatter(
        lax.optimization_barrier(partial_value.astype(jnp.bfloat16))
        .astype(jnp.float32)
        .astype(jnp.bfloat16),
        "head",
        scatter_dimension=0,
        tiled=True,
    )
    return (hidden_grad, enc_grad)


def solution(mesh):
    return jax.shard_map(
        shards,
        mesh=mesh,
        in_specs=(
            P("seq", "head"),
            P("seq", "head"),
            P("seq", None),
            P(None, "head"),
            P(None, "head"),
            P(None, "head"),
            P("head", None),
            P("seq", None),
            P("seq"),
        ),
        out_specs=(P(("seq", "head"), None), P("seq", "head")),
        check_vma=False,
    )
```

profile of v0, /device:TPU:0, one launch (start us, length us, event | category | flops | bytes accessed | tf_op | source)
XLA Modules:
  0.0 382.3 jit_solution(9835484429578831642)
XLA Ops:
  9.8 7.3 %all-to-all-start = ((s32[8,1,2]{2,1,0:T(1,128)}), s32[8,1,2]{2,1,0:T(1,128)S(1)}, u32[]{:S(2)}, u32[]{:S(2)}) async-start(s32[8,1,2]{2,1,0:T(1,128)} %bitcast), calls=%async_computation | async-start | bytes 8192 | tf_op jit(solution)/shard_map/all_to_all | solution.py:109
  26.1 4.3 %copy.82 = bf16[2,8,128,1024]{3,2,1,0:T(8,128)(2,1)} copy(bf16[2,8,128,1024]{3,1,2,0:T(8,128)(2,1)S(1)} %bitcast.71) | data formatting | bytes 8388608
  30.4 4.7 %all-to-all-start.1 = ((bf16[8,2,128,1024]{3,2,1,0:T(8,128)(2,1)}), bf16[8,2,128,1024]{3,2,1,0:T(8,128)(2,1)}, u32[]{:S(2)}, u32[]{:S(2)}) async-start(bf16[8,2,128,1024]{3,2,1,0:T(8,128)(2,1)} %bitcast.69), calls=%async_computation.1 | async-start | bytes 8388608 | tf_op jit(solution)/shard_map/all_to_all | solution.py:122
  37.3 9.5 %all-gather.5.cloned.1.call-done = bf16[512,4096]{1,0:T(8,128)(2,1)} async-done(((bf16[512,1024]{1,0:T(8,128)(2,1)}), bf16[512,4096]{1,0:T(8,128)(2,1)}) %all-gather.5.cloned.1.call-update) | async-done | bytes 4194320 | tf_op jit(solution)/shard_map/all_gather | solution.py:90
  46.8 5.8 %convolution_convert_fusion.4 = bf16[512,512]{1,0:T(8,128)(2,1)S(1)} fusion(bf16[512,4096]{1,0:T(8,128)(2,1)} %all-gather.5.cloned.1.call-done, bf16[512,4096]{1,0:T(8,128)(2,1)} %param.15), kind=kOutput, calls=%fused_computation.25 | convolution fusion | flops 2147745792 | bytes 8912896 | tf_op jit(solution)/shard_map/dot_general | solution.py:92
  52.7 30.1 %all-gather.3.cloned.1.call-done = bf16[512,4096]{1,0:T(8,128)(2,1)} async-done(((bf16[512,1024]{1,0:T(8,128)(2,1)}), bf16[512,4096]{1,0:T(8,128)(2,1)}) %all-gather.3.cloned.1.call-update) | async-done | bytes 4194320 | tf_op jit(solution)/shard_map/all_gather | solution.py:89
  82.8 5.8 %convolution_convert_fusion.5 = bf16[512,512]{1,0:T(8,128)(2,1)S(1)} fusion(bf16[512,4096]{1,0:T(8,128)(2,1)} %all-gather.3.cloned.1.call-done, bf16[4096,512]{1,0:T(8,128)(2,1)} %param.12), kind=kOutput, calls=%fused_computation.26 | convolution fusion | flops 2147745792 | bytes 8912896 | tf_op jit(solution)/shard_map/dot_general | solution.py:91
  89.9 37.4 %all-to-all-done.1 = bf16[8,2,128,1024]{3,2,1,0:T(8,128)(2,1)} async-done(((bf16[8,2,128,1024]{3,2,1,0:T(8,128)(2,1)}), bf16[8,2,128,1024]{3,2,1,0:T(8,128)(2,1)}, u32[]{:S(2)}, u32[]{:S(2)}) %all-to-all-start.1) | async-done | bytes 4194336 | tf_op jit(solution)/shard_map/all_to_all | solution.py:122
  127.3 4.5 %copy.83 = bf16[2,8,128,1024]{3,1,2,0:T(8,128)(2,1)S(1)} copy(bf16[2,8,128,1024]{3,2,1,0:T(8,128)(2,1)} %bitcast.11) | data formatting | bytes 8388608
  139.5 2.5 reshape.199
  145.4 7.4 %convert_bitcast_fusion = bf16[8,256,4,128]{1,3,2,0:T(8,128)(2,1)} fusion(bf16[8,64,4,128]{3,2,1,0:T(4,128)(2,1)} %concatenate.22, pred[8,64]{1,0:T(8,128)(4,1)} %add_compare_fusion, f32[8,4,64]{2,1,0:T(4,128)S(1)} %get-tuple-element.6, f32[8,4,64,256]{3,2,1,0:T(8,128)} %copy-done.3, pred[8,256]{1,0:T(8,128)(4,1)} %broadcast_bitcast_fusion), kind=kOutput, calls=%fused_computation.7 | convolution fusion | flops 138152192 | bytes 4729344 | tf_op jit(solution)/shard_map/chqk,cqhd->ckhd/dot_general | solution.py:57
  152.9 6.3 %fusion.25 = f32[8,64,4]{1,2,0:T(4,128)} fusion(bf16[8,256,4,128]{3,2,1,0:T(4,128)(2,1)S(1)} %copy-done.5, bf16[8,64,4,128]{3,2,1,0:T(4,128)(2,1)} %concatenate.22, pred[8,64]{1,0:T(8,128)(4,1)} %add_compare_fusion, f32[8,4,64]{2,1,0:T(4,128)S(1)} %get-tuple-element.6, f32[8,4,64,256]{3,2,1,0:T(8,128)} %copy-done.3, pred[8,256]{1,0:T(8,128)(4,1)} %broadcast_bitcast_fusion), kind=kOutput, calls=%fused_computation.30 | convolution fusion | flops 137888000 | bytes 4737536 | tf_op jit(solution)/shard_map/chqk,ckhd->cqhd/dot_general | solution.py:40
  159.2 2.8 copy.74
  164.1 3.3 multiply_convert_fusion.1
  171.8 4.5 %fusion.61 = bf16[2,8,128,1024]{2,1,0,3:T(8,128)(2,1)} fusion(bf16[16,128,512]{1,0,2:T(8,128)(2,1)} %reshape.191, bf16[16,128,512]{1,0,2:T(8,128)(2,1)} %reshape.190), kind=kLoop, calls=%fused_computation.81 | loop fusion | flops 2097152 | bytes 8388608
  176.3 7.8 %copy.86 = bf16[2,8,128,1024]{3,1,2,0:T(8,128)(2,1)} copy(bf16[2,8,128,1024]{2,1,0,3:T(8,128)(2,1)} %fusion.61) | data formatting | bytes 8388608
  184.2 3.5 convolution_convert_fusion
  190.1 96.7 %all_to_all.16 = bf16[8,2,128,1024]{3,2,1,0:T(8,128)(2,1)S(1)} all-to-all(bf16[8,2,128,1024]{3,2,1,0:T(8,128)(2,1)S(1)} %bitcast.72), channel_id=1, replica_groups=mesh['seq'=8,'head'=4] {'seq'}, dimensions={0} | all-to-all | bytes 8388608 | tf_op jit(solution)/shard_map/all_to_all | solution.py:146
  290.3 2.8 reshape.195
  293.1 3.1 fusion.32
  296.2 3.0 convolution_add_fusion
  302.0 4.3 %convolution_convert_fusion.3 = bf16[512,4096]{1,0:T(8,128)(2,1)} fusion(bf16[4096,512]{1,0:T(8,128)(2,1)S(1)} %copy-done.13, bf16[449,512]{1,0:T(8,128)(2,1)S(1)} %slice.51, bf16[63,512]{1,0:T(8,128)(2,1)S(1)} %slice.50), kind=kOutput, calls=%fused_computation.4 | convolution fusion | flops 2150629376 | bytes 8912896 | tf_op jit(solution)/shard_map/dot_general | solution.py:169
  306.3 21.7 %reduce-scatter.5.cloned.1.call-done = f32[512,224]{0,1:T(8,128)} async-done(((f32[512,896]{0,1:T(8,128)}), f32[512,224]{0,1:T(8,128)}) %reduce-scatter.5.cloned.1.call-update) | async-done | bytes 458768 | tf_op jit(solution)/shard_map/reduce_scatter | solution.py:166
  329.8 45.8 %reduce-scatter.3.cloned.1.call-done = bf16[128,4096]{1,0:T(8,128)(2,1)} async-done(((bf16[512,4096]{1,0:T(8,128)(2,1)}), bf16[128,4096]{1,0:T(8,128)(2,1)}) %reduce-scatter.3.cloned.1.call-update) | async-done | bytes 1048592 | tf_op jit(solution)/shard_map/reduce_scatter | solution.py:172
  (89 shorter events, 43.0 us)
Async XLA Ops:
  7.2 12.4 %copy-start = (bf16[896,512]{1,0:T(8,128)(2,1)S(1)}, bf16[896,512]{1,0:T(8,128)(2,1)}, u32[]{:S(2)}) copy-start(bf16[896,512]{1,0:T(8,128)(2,1)} %param.13) | copy-start | bytes 2752516
  7.2 12.4 %copy-start.14 = (bf16[512,896]{1,0:T(8,128)(2,1)S(1)}, bf16[512,896]{1,0:T(8,128)(2,1)}, u32[]{:S(2)}) copy-start(bf16[512,896]{1,0:T(8,128)(2,1)} %param.11) | copy-start | bytes 2752516
  7.2 39.6 %all-gather.5.cloned.1.call-start = ((), (), s32[]{:S(2)}) async-start(), calls=%async_computation.6 | async-start | bytes 5242880 | tf_op jit(solution)/shard_map/all_gather | solution.py:90
  9.0 122.8 %copy-start.11 = (s32[16]{0:T(128)}, s32[16]{0:T(128)S(1)}, u32[]{:S(2)}) copy-start(s32[16]{0:T(128)S(1)} %multiply_add_fusion) | copy-start | bytes 196
  9.8 13.7 %all-to-all-start = ((s32[8,1,2]{2,1,0:T(1,128)}), s32[8,1,2]{2,1,0:T(1,128)S(1)}, u32[]{:S(2)}, u32[]{:S(2)}) async-start(s32[8,1,2]{2,1,0:T(1,128)} %bitcast), calls=%async_computation | async-start | bytes 8192 | tf_op jit(solution)/shard_map/all_to_all | solution.py:109
  24.8 1.3 copy-start.9
  30.4 6.2 %copy-start.15 = (s32[8]{0:T(128)S(1)}, s32[8]{0:T(128)}, u32[]{:S(2)}) copy-start(s32[8]{0:T(128)} %param.17) | copy-start | bytes 100
  30.4 96.9 %all-to-all-start.1 = ((bf16[8,2,128,1024]{3,2,1,0:T(8,128)(2,1)}), bf16[8,2,128,1024]{3,2,1,0:T(8,128)(2,1)}, u32[]{:S(2)}, u32[]{:S(2)}) async-start(bf16[8,2,128,1024]{3,2,1,0:T(8,128)(2,1)} %bitcast.69), calls=%async_computation.1 | async-start | bytes 8388608 | tf_op jit(solution)/shard_map/all_to_all | solution.py:122
  35.1 47.7 %all-gather.3.cloned.1.call-start = ((), (), s32[]{:S(2)}) async-start(), calls=%async_computation.5 | async-start | bytes 5242880 | tf_op jit(solution)/shard_map/all_gather | solution.py:89
  35.9 292.2 %reduce-scatter.5.cloned.1.call-start = ((), (), s32[]{:S(2)}) async-start(), calls=%async_computation.8 | async-start | bytes 2293760 | tf_op jit(solution)/shard_map/reduce_scatter | solution.py:166
  142.1 1.4 copy-start.1
  142.1 1.4 copy-start.8
  143.4 2.0 copy-start.3
  145.4 7.5 %copy-start.5 = (bf16[8,256,4,128]{3,2,1,0:T(4,128)(2,1)S(1)}, bf16[8,256,4,128]{3,2,1,0:T(4,128)(2,1)}, u32[]{:S(2)}) copy-start(bf16[8,256,4,128]{3,2,1,0:T(4,128)(2,1)} %reshape.200) | copy-start | bytes 6291460
  167.4 1.0 copy-start.6
  176.3 7.8 %copy-start.12 = (s32[16]{0:T(128)S(1)}, s32[16]{0:T(128)}, u32[]{:S(2)}) copy-start(s32[16]{0:T(128)} %copy-done.11) | copy-start | bytes 196
  286.8 2.3 copy-start.10
  293.1 3.1 copy-start.4
  293.1 3.1 copy-start.7
  296.2 3.3 copy-start.2
  299.2 76.4 %reduce-scatter.3.cloned.1.call-start = ((), (), s32[]{:S(2)}) async-start(), calls=%async_computation.7 | async-start | bytes 5242880 | tf_op jit(solution)/shard_map/reduce_scatter | solution.py:172
  299.5 2.5 copy-start.13
Sparse Core Ops, SparseCore 0:
  9.6 37.1 all-gather.4
  48.3 34.4 all-gather.2
  299.4 28.6 reduce-scatter.4
  331.0 44.5 reduce-scatter.2
where the time goes:
time: 388 us; the launch traced here: 382 us
  waiting for transfers between devices  148 us (38%)
  blocking collectives  96.7 us (25%)
  matrix products  52.9 us (14%)
  local copies, waits for them, and re-layouts  48.1 us (12%)
  between operations  14.3 us (4%)
  starting transfers between devices  12.5 us (3%)
  other arithmetic  10 us (3%)
    all_to_all x1, blocking collectives, shards(): lax.all_to_all(returning.reshape(seq_count, slot_cap, RET, 2 * columns),...  96.7 us
    reduce_scatter x1, waiting for transfers between devices, shards(): lax.psum_scatter(lax.optimization_barrier(partial_value.astype(jnp.bfloat...  45.8 us
    all_to_all x1, waiting for transfers between devices, shards(): lax.all_to_all(outgoing.reshape(seq_count, slot_cap, RET, 2 * columns), '...  37.4 us
    all_gather x1, waiting for transfers between devices, shards(): hidden_piece = lax.all_gather(hidden_states, 'head', axis=1, tiled=True)  30.1 us
    unnamed x40, local copies, waits for them, and re-layouts  25.3 us
    reduce_scatter x1, waiting for transfers between devices, shards(): lax.psum_scatter(enc_part, 'head', scatter_dimension=1, tiled=True)  21.7 us
    all_gather x1, waiting for transfers between devices, shards(): grad_piece = lax.all_gather(out_grad, 'head', axis=1, tiled=True)  9.47 us
  transfers between devices with their start and end apart: 6, of which 6 were waited for; matrix products, arithmetic and copies ran while one was open for 9% of the time, Pallas kernels for 0%

commit v1 on v0

v1 whole, which is shorter than its diff:
```python
import functools
import math

import jax
import jax.numpy as jnp
from jax import lax
from jax.experimental import pallas as pl
from jax.experimental.pallas import tpu as pltpu
from jax.sharding import PartitionSpec as P


HD = 128
SPAN = 64
NEIGH = 2
RET = 128
CORES = 2
CAP = 2
HALF = RET // CORES


BF16 = jnp.bfloat16
F32 = jnp.float32
F16 = jnp.float16
NT = (((1,), (1,)), ((), ()))
TN = (((0,), (0,)), ((), ()))
VM = pltpu.MemorySpace.VMEM
SM = pltpu.MemorySpace.SMEM


def swap(value, axis, distance):
    count = lax.axis_size(axis)
    return lax.ppermute(value, axis, [(i, i ^ distance) for i in range(count)])


def after(value, *others):
    return lax.optimization_barrier((value,) + others)[0]


def table_by_distance(row, count):
    table = row
    distance = 1
    while distance < count:
        table = jnp.concatenate([table, swap(table, "seq", distance)], axis=0)
        distance *= 2
    return table


def pack(value, bound):
    return (value * (32768.0 / bound)).astype(F16)


def unpack(value, bound):
    return value.astype(F32) * (bound / 32768.0)


def slots_of(named, per_shard):
    slots = [jnp.int32(0)] * CAP
    seen = jnp.int32(0)
    for record in range(per_shard):
        bit = (named >> record) & 1
        for slot in range(CAP):
            slots[slot] = jnp.where((bit == 1) & (seen == slot), record, slots[slot])
        seen = seen + bit
    return slots


def request_kernel(place_ref, ids_ref, enc_ref, asked_ref, *blocks, seq_count, per_shard):
    me = place_ref[0]
    core = place_ref[1] % CORES
    entries = ids_ref.shape[0] * ids_ref.shape[1] // seq_count
    width = ids_ref.shape[1]
    for distance in reversed(range(seq_count)):
        named = jnp.int32(0)
        for entry in range(entries):
            at = distance * entries + entry
            record = ids_ref[at // width, at % width]
            hit = record // per_shard == me
            named = named | jnp.where(hit, 1 << (record % per_shard), 0)
        slots = slots_of(named, per_shard)
        for slot in range(CAP):
            start = pl.multiple_of(slots[slot] * RET + core * HALF, HALF)
            blocks[distance][slot] = enc_ref[pl.ds(start, HALF), :]
            if distance == 0:
                other = pl.multiple_of(slots[slot] * RET + (1 - core) * HALF, HALF)
                blocks[seq_count][slot] = enc_ref[pl.ds(other, HALF), :]
        chosen = slots[0]
        for slot in range(1, CAP):
            chosen = jnp.where(core == slot, slots[slot], chosen)
        asked_ref[distance] = chosen


def request(place, ids_table, encodings, seq_count):
    per_shard = encodings.shape[0] // RET
    block = jax.ShapeDtypeStruct((CAP, HALF, encodings.shape[1]), BF16)
    return pl.pallas_call(
        functools.partial(request_kernel, seq_count=seq_count, per_shard=per_shard),
        out_shape=[jax.ShapeDtypeStruct((seq_count,), jnp.int32)] + [block] * (seq_count + 1),
        in_specs=[pl.BlockSpec(memory_space=SM)] * 2 + [pl.BlockSpec(memory_space=VM)],
        out_specs=[pl.BlockSpec(memory_space=SM)]
        + [pl.BlockSpec(memory_space=VM)] * (seq_count + 1),
        cost_estimate=pl.CostEstimate(
            flops=0, transcendentals=0, bytes_accessed=4 * encodings.size * 2
        ),
        name="request",
    )(place, ids_table, encodings)


def plan_kernel(place_ref, ids_ref, plan_ref, *, per_shard):
    me = place_ref[0]
    rows, cols = ids_ref.shape
    entries = rows * cols
    records = [ids_ref[entry // cols, entry % cols] for entry in range(entries)]
    for entry in range(entries):
        owner = records[entry] // per_shard
        local = records[entry] % per_shard
        below = jnp.int32(0)
        earlier = jnp.int32(0)
        for other in range(entries):
            same = records[other] // per_shard == owner
            below = below | jnp.where(same, 1 << (records[other] % per_shard), 0)
            if other < entry:
                earlier = earlier | jnp.where(records[other] == records[entry], 1, 0)
        below = below & ((1 << local) - 1)
        rank = jnp.int32(0)
        for bit_at in range(per_shard):
            rank = rank + ((below >> bit_at) & 1)
        plan_ref[entry] = owner ^ me
        plan_ref[entries + entry] = rank
        plan_ref[2 * entries + entry] = earlier


def plan_entries(place, ids, per_shard):
    return pl.pallas_call(
        functools.partial(plan_kernel, per_shard=per_shard),
        out_shape=jax.ShapeDtypeStruct((3 * ids.size,), jnp.int32),
        in_specs=[pl.BlockSpec(memory_space=SM)] * 2,
        out_specs=pl.BlockSpec(memory_space=SM),
        cost_estimate=pl.CostEstimate(flops=0, transcendentals=0, bytes_accessed=1 << 20),
        name="plan",
    )(place, ids)


def project_kernel(place_ref, *refs, count):
    pieces = refs[: 2 * count]
    wk_ref, wv_ref = refs[2 * count : 2 * count + 2]
    key_ref, value_ref, rows = refs[-3:]
    core = place_ref[1] % CORES

    @pl.when(pl.program_id(0) == 0)
    def _():
        for block in range(count):
            for source, half in ((pieces[2 * block], core), (pieces[2 * block + 1], 1 - core)):
                for slot in range(CAP):
                    at = pl.multiple_of((block * CAP + slot) * RET + half * HALF, HALF)
                    rows[pl.ds(at, HALF), :] = source[slot]

    for weight, target in ((wk_ref, key_ref), (wv_ref, value_ref)):
        target[...] = jnp.dot(rows[...], weight[...], preferred_element_type=F32).astype(BF16)


def project(place, pieces, w_key, w_value, held, group, groups):
    depth, columns = w_key.shape
    count = len(pieces) // 2
    height = count * CAP * RET
    wide = min(columns, 256)
    shape = jax.ShapeDtypeStruct((groups * height, columns), BF16)
    whole = lambda a: pl.BlockSpec(a.shape, lambda i: (0,) * a.ndim)
    weight_spec = pl.BlockSpec((depth, wide), lambda i: (0, i))
    out_spec = pl.BlockSpec((height, wide), lambda i: (group, i))
    extra = list(held) if held is not None else []
    args = len(pieces) + 2
    return pl.pallas_call(
        functools.partial(project_kernel, count=count),
        grid=(columns // wide,),
        out_shape=[shape, shape],
        in_specs=[pl.BlockSpec(memory_space=SM)]
        + [whole(a) for a in pieces]
        + [weight_spec] * 2
        + [pl.BlockSpec(memory_space=pl.ANY)] * len(extra),
        out_specs=[out_spec, out_spec],
        scratch_shapes=[pltpu.VMEM((height, depth), BF16)],
        input_output_aliases={args + 1: 0, args + 2: 1} if extra else {},
        cost_estimate=pl.CostEstimate(
            flops=4 * height * w_key.size,
            transcendentals=0,
            bytes_accessed=4 * (w_key.size + height * columns),
        ),
        name="project",
    )(place, *pieces, w_key, w_value, *extra)


def attend_kernel(
    place_ref,
    plan_ref,
    counts_ref,
    tops_ref,
    q_ref,
    g_ref,
    k_ref,
    v_ref,
    ready_query,
    ready_pair,
    qg_mine,
    qg_theirs,
    bound_ref,
    mine_far,
    mine_near,
    theirs_far,
    theirs_near,
    q_rows,
    g_rows,
    qg_rows,
    kv_pair,
    kv_all,
    highest,
    sems,
):
    core = place_ref[1] % CORES
    rows, columns = q_ref.shape
    heads = columns // HD
    shift = SPAN - 1
    spans = rows // SPAN
    entries = spans * NEIGH
    seq_count = kv_all.shape[0] // (CAP * RET)
    full = rows - SPAN
    scale = 1.0 / math.sqrt(HD)
    for source, target in ((q_ref, q_rows), (g_ref, g_rows)):
        target[0:full, :] = source[shift : shift + full, :].astype(BF16)
        first = lax.broadcasted_iota(jnp.int32, (SPAN, columns), 0) == 0
        last = jnp.broadcast_to(source[rows - 1 : rows, :], (SPAN, columns))
        target[full:rows, :] = jnp.where(first, last, 0.0).astype(BF16)
    kv_all[...] = jnp.zeros_like(kv_all)
    highest[...] = jnp.zeros_like(highest)

    def fold(value):
        return jnp.max(jnp.abs(value).reshape(-1, 8, HD), axis=0)

    def one_span(span, carry):
        base = pl.multiple_of(span * SPAN, SPAN)
        two = counts_ref[span] > 1
        dist = [plan_ref[span * NEIGH + n] for n in range(NEIGH)]
        rank = [plan_ref[entries + span * NEIGH + n] for n in range(NEIGH)]
        again = [plan_ref[2 * entries + span * NEIGH + n] for n in range(NEIGH)]
        key_at = [pl.multiple_of((dist[n] * CAP + rank[n]) * RET, RET) for n in range(NEIGH)]
        column_at = lax.broadcasted_iota(jnp.int32, (SPAN, NEIGH * RET), 1)
        in_use = (column_at < RET) | two
        each = range(heads)
        lanes = [slice(head * HD, (head + 1) * HD) for head in each]
        q = [q_rows[pl.ds(base, SPAN), lanes[h]] for h in each]
        g = [g_rows[pl.ds(base, SPAN), lanes[h]] for h in each]
        k = [
            jnp.concatenate([k_ref[pl.ds(at, RET), lanes[h]] for at in key_at], axis=0)
            for h in each
        ]
        v = [
            jnp.concatenate([v_ref[pl.ds(at, RET), lanes[h]] for at in key_at], axis=0)
            for h in each
        ]
        scores = [
            lax.dot_general(q[h], k[h], NT, preferred_element_type=F32) * scale for h in each
        ]
        prob = [lax.dot_general(g[h], v[h], NT, preferred_element_type=F32) for h in each]
        scores = [jnp.where(in_use, scores[h], -jnp.inf) for h in each]
        top = [jnp.max(scores[h], axis=-1, keepdims=True) for h in each]
        exponent = [jnp.exp(scores[h] - top[h]) for h in each]
        soft = [exponent[h] / jnp.sum(exponent[h], axis=-1, keepdims=True) for h in each]
        low = [soft[h].astype(BF16) for h in each]
        out = [jnp.dot(low[h], v[h], preferred_element_type=F32) for h in each]
        vg = [lax.dot_general(low[h], g[h], TN, preferred_element_type=F32) for h in each]
        delta = [jnp.sum(g[h].astype(F32) * out[h], axis=-1, keepdims=True) for h in each]
        score_low = [(soft[h] * (prob[h] - delta[h])).astype(BF16) for h in each]
        qg = [jnp.dot(score_low[h], k[h], preferred_element_type=F32) * scale for h in each]
        kg = [
            lax.dot_general(score_low[h], q[h], TN, preferred_element_type=F32) * scale
            for h in each
        ]
        for h in each:
            qg_rows[pl.ds(base, SPAN), lanes[h]] = qg[h]
            kv_pair[:, lanes[h]] = kg[h].astype(BF16)
            kv_pair[:, columns + h * HD : columns + (h + 1) * HD] = vg[h].astype(BF16)
        for at, made in enumerate((qg, kg, vg)):
            most = highest[at]
            for h in each:
                most = jnp.maximum(most, fold(made[h]))
            highest[at] = most
        for n in range(NEIGH):
            made = slice(n * RET, (n + 1) * RET)
            which = jnp.where(rank[n] == core, 0, 1)
            at = pl.multiple_of((which * seq_count + dist[n]) * RET, RET)

            @pl.when(again[n] == 0)
            def _():
                kv_all[pl.ds(at, RET), :] = kv_pair[made, :]

            @pl.when(again[n] != 0)
            def _():
                total = kv_all[pl.ds(at, RET), :].astype(F32) + kv_pair[made, :].astype(F32)
                kv_all[pl.ds(at, RET), :] = total.astype(BF16)

        return carry

    lax.fori_loop(0, spans, one_span, 0)
    half = seq_count // 2 * RET
    copies = []
    for at, target in enumerate((mine_near, mine_far, theirs_near, theirs_far)):
        copies.append(
            pltpu.make_async_copy(kv_all.at[pl.ds(at * half, half), :], target, sems.at[at])
        )
    for copy in copies:
        copy.start()
    moved = jnp.concatenate(
        [jnp.zeros((shift, columns), F32), qg_rows[0 : rows - shift, :]], axis=0
    )
    qg_rows[...] = moved
    pieces, take = qg_mine.shape[:2]
    for piece in range(pieces):
        for target, which in ((qg_mine, core), (qg_theirs, 1 - core)):
            at = pl.multiple_of((piece * CORES + which) * take, take)
            target[piece] = qg_rows[pl.ds(at, take), :].astype(BF16)
    most = [jnp.max(highest[at]) for at in range(3)]
    hidden_bound = most[0] * tops_ref[0] * columns
    enc_bound = (most[1] * tops_ref[1] + most[2] * tops_ref[2]) * (columns * entries)
    upper = lax.broadcasted_iota(jnp.int32, bound_ref.shape, 0) < 4
    bound_ref[...] = jnp.where(upper, hidden_bound, enc_bound) * 1.03125 + 1e-30
    for copy in copies:
        copy.wait()


def attend(place, plan, counts, tops, q, g, key_rows, value_rows, ready, chips):
    rows, columns = q.shape
    height = key_rows.shape[0]
    take = rows // (chips * CORES)
    qg = jax.ShapeDtypeStruct((chips, take, columns), BF16)
    kv = jax.ShapeDtypeStruct((height // 4, 2 * columns), BF16)
    bound = jax.ShapeDtypeStruct((8, HD), F32)
    flops = 6 * 2 * rows * NEIGH * RET * columns
    anywhere = pl.BlockSpec(memory_space=pl.ANY)
    return pl.pallas_call(
        attend_kernel,
        out_shape=[qg, qg, bound, kv, kv, kv, kv],
        in_specs=[pl.BlockSpec(memory_space=SM)] * 4
        + [pl.BlockSpec(memory_space=VM)] * 4
        + [anywhere] * 2,
        out_specs=[pl.BlockSpec(memory_space=VM)] * 3 + [anywhere] * 4,
        scratch_shapes=[
            pltpu.VMEM((rows, columns), BF16),
            pltpu.VMEM((rows, columns), BF16),
            pltpu.VMEM((rows, columns), F32),
            pltpu.VMEM((NEIGH * RET, 2 * columns), BF16),
            pltpu.VMEM((height, 2 * columns), BF16),
            pltpu.VMEM((3, 8, HD), F32),
            pltpu.SemaphoreType.DMA((4,)),
        ],
        compiler_params=pltpu.CompilerParams(vmem_limit_bytes=40 << 20),
        cost_estimate=pl.CostEstimate(
            flops=8 * flops,
            transcendentals=rows * NEIGH * RET * columns // HD,
            bytes_accessed=8 * q.size + 8 * key_rows.size,
        ),
        name="attend",
    )(place, plan, counts, tops, q, g, key_rows, value_rows, *ready)


def collect_kernel(asked_ref, place_ref, *refs):
    blocks = refs[:-3]
    mine_ref, theirs_ref, total = refs[-3:]
    core = place_ref[1] % CORES
    total[...] = jnp.zeros_like(total)
    for distance, block in enumerate(blocks):
        at = pl.multiple_of(asked_ref[distance] * RET, RET)
        total[:, pl.ds(at, RET)] += block[...].astype(F32)
    take = mine_ref.shape[0]
    for target, which in ((mine_ref, core), (theirs_ref, 1 - core)):
        target[...] = total[pl.ds(pl.multiple_of(which * take, take), take), :]


def collect(asked, place, blocks, per_shard):
    height = blocks[0].shape[0]
    half = jax.ShapeDtypeStruct((height // CORES, per_shard * RET), F32)
    return pl.pallas_call(
        collect_kernel,
        out_shape=[half, half],
        in_specs=[pl.BlockSpec(memory_space=SM)] * 2
        + [pl.BlockSpec(memory_space=VM)] * len(blocks),
        out_specs=[pl.BlockSpec(memory_space=VM)] * 2,
        scratch_shapes=[pltpu.VMEM((height, per_shard * RET), F32)],
        cost_estimate=pl.CostEstimate(
            flops=2 * len(blocks) * blocks[0].size,
            transcendentals=0,
            bytes_accessed=4 * len(blocks) * blocks[0].size,
        ),
        name="collect",
    )(asked, place, *blocks)


def shards(
    hidden_states,
    out_grad,
    encodings,
    w_query,
    w_key,
    w_value,
    w_out,
    neighbour_ids,
    neighbour_counts,
):
    seq_count = lax.axis_size("seq")
    head_count = lax.axis_size("head")
    chips = head_count // CORES
    seq_at = lax.axis_index("seq")
    head_at = lax.axis_index("head")
    chip_at = head_at // CORES
    place = jnp.stack([seq_at, head_at]).astype(jnp.int32)
    per_shard = encodings.shape[0] // RET
    features = hidden_states.shape[1]
    width = encodings.shape[1]

    far = [(hidden_states, out_grad)]
    for step in range(1, chips):
        far.append(
            (
                swap(hidden_states, "head", step * CORES),
                swap(out_grad, "head", step * CORES),
            )
        )
    ids_table = table_by_distance(neighbour_ids.reshape(1, -1), seq_count)
    asked, *blocks = request(place, ids_table, encodings, seq_count)
    own_half = blocks.pop()
    mine = [None] * seq_count
    for distance in reversed(range(1, seq_count)):
        mine[distance] = swap(blocks[distance], "seq", distance)
    pieces = [(blocks[0], own_half)]
    for distance in range(1, seq_count):
        pieces.append((mine[distance], swap(mine[distance], "head", 1)))
    plan = plan_entries(after(place, asked), neighbour_ids, per_shard)

    w_query_near = swap(w_query, "head", 1)
    w_pair = jnp.concatenate([after(w_key, asked), w_value], axis=1)
    w_pair_near = swap(w_pair, "head", 1)
    late = after((w_query, w_key, w_value), asked)
    tops = jnp.stack([jnp.max(jnp.abs(w)).astype(F32) for w in late])

    held = None
    groups = 2
    per_group = seq_count // groups
    for group in range(groups):
        chosen = pieces[group * per_group : (group + 1) * per_group]
        flat = [piece for pair in chosen for piece in pair]
        held = project(place, flat, w_key, w_value, held, group, groups)
    key_rows, value_rows = held

    query_sum = jnp.zeros((), F32)
    grad_sum = jnp.zeros((), F32)
    for step in range(chips):
        for side in range(CORES):
            hidden_piece, grad_piece = far[step]
            if side:
                hidden_piece = swap(hidden_piece, "head", 1)
                grad_piece = swap(grad_piece, "head", 1)
            elif step == 0:
                hidden_piece, grad_piece = after((hidden_piece, grad_piece), asked)
            block_at = (head_at ^ (step * CORES + side)) * features
            query_sum = query_sum + jnp.dot(
                hidden_piece,
                lax.dynamic_slice_in_dim(w_query, block_at, features, 0),
                preferred_element_type=F32,
            )
            grad_sum = grad_sum + lax.dot_general(
                grad_piece,
                lax.dynamic_slice_in_dim(w_out, block_at, features, 1),
                NT,
                preferred_element_type=F32,
            )

    qg_mine, qg_theirs, bound, mine_far, mine_near, theirs_far, theirs_near = attend(
        place,
        plan,
        neighbour_counts,
        tops,
        query_sum,
        grad_sum,
        key_rows,
        value_rows,
        (w_query_near, w_pair_near),
        chips,
    )
    far_near = swap(theirs_far, "head", 1)
    total_bound = bound
    for d in range(1, head_count):
        total_bound = total_bound + swap(bound, "head", d)
    qg_near = swap(qg_theirs, "head", 1)
    near_near = swap(theirs_near, "head", 1)
    hidden_bound = total_bound[0, 0]
    enc_bound = total_bound[4, 0]

    strip = width // chips

    def enc_strip(step, kv, near_kv, *earlier):
        at = (chip_at ^ step) * strip
        own = lax.dynamic_slice_in_dim(w_pair, at, strip, 0)
        near = lax.dynamic_slice_in_dim(w_pair_near, at, strip, 0)
        if earlier:
            kv = after(kv, *earlier)
        return lax.dot_general(own, kv, NT, preferred_element_type=F32) + lax.dot_general(
            near, near_kv, NT, preferred_element_type=F32
        )

    halves = ((mine_far, far_near, seq_count // 2), (mine_near, near_near, 0))
    packed = []
    sent = []
    for kv, near_kv, first in halves:
        made = [
            pack(enc_strip(step, kv, near_kv, *packed), enc_bound) for step in range(1, chips)
        ]
        packed = packed + made
        sent.append([swap(made[step - 1], "head", step * CORES) for step in range(1, chips)])
    take = qg_mine.shape[1]
    rows_of = lambda v: v.reshape(chips * take, v.shape[2])
    own_part = lax.dot_general(
        after(rows_of(qg_mine), *packed), w_query, NT, preferred_element_type=F32
    )
    near_part = lax.dot_general(
        rows_of(qg_near), w_query_near, NT, preferred_element_type=F32
    )
    own_part, near_part = lax.optimization_barrier(
        (own_part.astype(BF16), near_part.astype(BF16))
    )

    def hidden_rows(step):
        at = (chip_at ^ step) * take
        return lax.dynamic_slice_in_dim(own_part, at, take, 0).astype(
            F32
        ) + lax.dynamic_slice_in_dim(near_part, at, take, 0).astype(F32)

    hidden_packed = [pack(hidden_rows(step), hidden_bound) for step in range(1, chips)]
    hidden_sent = [swap(hidden_packed[step - 1], "head", step * CORES) for step in range(1, chips)]
    total_table = table_by_distance(after(total_bound, *packed)[4:5, :], seq_count)

    back = [None] * seq_count
    done = hidden_packed
    for (kv, near_kv, first), arrived in zip(halves, sent):
        enc_sum = lax.optimization_barrier(enc_strip(0, kv, near_kv, *done))
        for piece in arrived:
            enc_sum = enc_sum + unpack(piece, enc_bound)
        made = []
        for distance in range(first, first + seq_count // 2):
            at = (distance - first) * RET
            piece = enc_sum[:, at : at + RET]
            if distance > 0:
                made.append(pack(piece, enc_bound))
                piece = swap(made[-1], "seq", distance)
                piece = unpack(piece, total_table[distance, 0])
            back[distance] = piece
        done = made
    enc_mine, enc_theirs = collect(asked, place, back, per_shard)
    enc_grad = (enc_mine + swap(enc_theirs, "head", 1)).T.astype(BF16)

    hidden_sum = hidden_rows(0)
    for piece in hidden_sent:
        hidden_sum = hidden_sum + unpack(piece, hidden_bound)
    return (hidden_sum.astype(BF16), enc_grad)


def solution(mesh):
    return jax.shard_map(
        shards,
        mesh=mesh,
        in_specs=(
            P("seq", "head"),
            P("seq", "head"),
            P("seq", None),
            P(None, "head"),
            P(None, "head"),
            P(None, "head"),
            P("head", None),
            P("seq", None),
            P("seq"),
        ),
        out_specs=(P(("seq", "head"), None), P("seq", "head")),
        check_vma=False,
    )
```

time: 388 us -> 215 us (0.55); the launches traced: 382 us -> 214 us
  waiting for transfers between devices: 148 us -> 50.2 us
  blocking collectives: 96.7 us -> 0 us
  starting transfers between devices: 12.5 us -> 63.1 us
  local copies, waits for them, and re-layouts: 48.1 us -> 9.04 us
  Pallas kernels: 0 us -> 29.1 us
  matrix products: 52.9 us -> 35.3 us
  other arithmetic: 10 us -> 19.8 us
  between operations: 14.3 us -> 7.55 us
    all_to_all x1 -> x0, blocking collectives: 96.7 us -> none  [shards(): lax.all_to_all(returning.reshape(seq_count, slot_cap, RET, 2 * columns),...]
    reduce_scatter x2 -> x0, waiting for transfers between devices: 67.5 us -> none  [the longest x1 45.8 us: shards(): lax.psum_scatter(lax.optimization_barrier(partial_value.astype(jnp.bfloat...]
    ppermute x0 -> x45, starting transfers between devices: none -> 63.1 us  [swap(): return lax.ppermute(value, axis, [(i, i ^ distance) for i in range(count)])]
    ppermute x0 -> x45, waiting for transfers between devices: none -> 50.2 us  [swap(): return lax.ppermute(value, axis, [(i, i ^ distance) for i in range(count)])]
    all_gather x2 -> x0, waiting for transfers between devices: 39.6 us -> none  [the longest x1 30.1 us: shards(): hidden_piece = lax.all_gather(hidden_states, 'head', axis=1, tiled=True)]
    all_to_all x2 -> x0, waiting for transfers between devices: 39.2 us -> none  [the longest x1 37.4 us: shards(): lax.all_to_all(outgoing.reshape(seq_count, slot_cap, RET, 2 * columns), '...]
    pallas_call x0 -> x6, Pallas kernels: none -> 29.1 us  [the longest x2 11.1 us: project(): pl.pallas_call(functools.partial(project_kernel, count=count), grid=(colu...]
    unnamed x40 -> x62, local copies, waits for them, and re-layouts: 25.3 us -> 6.16 us
  transfers between devices with their start and end apart: 6 -> 45, of which waited for: 6 -> 16; matrix products, arithmetic and copies ran while one was open for 9% -> 26% of each run, Pallas kernels for 0% -> 9%
where the time goes in v1:
time: 215 us; the launch traced here: 214 us
  starting transfers between devices  63.1 us (29%)
  waiting for transfers between devices  50.2 us (23%)
  matrix products  35.3 us (16%)
  Pallas kernels  29.1 us (14%)
  other arithmetic  19.8 us (9%)
  local copies, waits for them, and re-layouts  9.04 us (4%)
  between operations  7.55 us (4%)
    ppermute x45, starting transfers between devices, swap(): return lax.ppermute(value, axis, [(i, i ^ distance) for i in range(count)])  63.1 us
    ppermute x45, waiting for transfers between devices, swap(): return lax.ppermute(value, axis, [(i, i ^ distance) for i in range(count)])  50.2 us
    pallas_call x2, Pallas kernels, project(): pl.pallas_call(functools.partial(project_kernel, count=count), grid=(colu...  11.1 us
    pallas_call x1, Pallas kernels, attend(): pl.pallas_call(attend_kernel, out_shape=[qg, qg, bound, kv, kv, kv, kv],...  9.79 us
    dot_general x4, matrix products, shards(): lax.dot_general(grad_piece, lax.dynamic_slice_in_dim(w_out, block_at, fea...  8.43 us
    dot_general x4, matrix products, shards(): jnp.dot(hidden_piece, lax.dynamic_slice_in_dim(w_query, block_at, feature...  8.13 us
    dot_general x4, matrix products, enc_strip(): lax.dot_general(own, kv, NT, preferred_element_type=F32)  7.8 us
    unnamed x62, local copies, waits for them, and re-layouts  6.16 us
  transfers between devices with their start and end apart: 45, of which 16 were waited for; matrix products, arithmetic and copies ran while one was open for 26% of the time, Pallas kernels for 9%

profile of v1, /device:TPU:0, one launch (start us, length us, event | category | flops | bytes accessed | tf_op | source)
XLA Modules:
  0.0 214.0 jit_solution(1309439430366072386)
XLA Ops:
  1.5 3.0 %collective-permute-start = (s32[1,16]{1,0:T(1,128)S(1)}, s32[1,16]{1,0:T(1,128)S(1)}, u32[]{:S(2)}, u32[]{:S(2)}) collective-permute-start(s32[1,16]{1,0:T(1,128)S(1)} %reshape.35), channel_id=1, source_target_pairs={{0,4},{4,0},{8,12},{12,8},{16,20},{20,16},{24,28},{28,24},{1,5},{5... | collective-permute-start | bytes 200 | tf_op jit(solution)/shard_map/ppermute | solution.py:32
  9.7 3.1 %collective-permute-start.2 = (s32[4,16]{1,0:T(4,128)S(1)}, s32[4,16]{1,0:T(4,128)S(1)}, u32[]{:S(2)}, u32[]{:S(2)}) collective-permute-start(s32[4,16]{1,0:T(4,128)S(1)} %pad_add_fusion.1), channel_id=1, source_target_pairs={{0,16},{4,20},{8,24},{12,28},{16,0},{20,4},{24,8},{28,12},{1,17},{... | collective-permute-start | bytes 776 | tf_op jit(solution)/shard_map/ppermute | solution.py:32
  15.0 3.4 %request.1 = (s32[8]{0:T(128)}, bf16[2,64,896]{2,1,0:T(8,128)(2,1)}, bf16[2,64,896]{2,1,0:T(8,128)(2,1)}, bf16[2,64,896]{2,1,0:T(8,128)(2,1)}, bf16[2,64,896]{2,...) custom-call(s32[2]{0:T(128)} %pad_add_fusion.3.place_ref, ...), custom_call_target="tpu_custom_call" | custom-call | bytes 3670016 | tf_op jit(solution)/shard_map/request/pallas_call | solution.py:95
  22.0 2.9 %collective-permute-start.9 = (bf16[2,64,896]{2,1,0:T(8,128)(2,1)}, bf16[2,64,896]{2,1,0:T(8,128)(2,1)S(1)}, u32[]{:S(2)}, u32[]{:S(2)}) collective-permute-start(bf16[2,64,896]{2,1,0:T(8,128)(2,1)} %get-tuple-element.46), channel_id=1, source_target_pairs={{0,16},{4,20},{8,24},{12,28},{16,0},{20,4},{24,8},{28,12},{1,17},{... | collective-permute-start | bytes 688136 | tf_op jit(solution)/shard_map/ppermute | solution.py:32
  26.4 3.7 %collective-permute-start.11 = (bf16[2,64,896]{2,1,0:T(8,128)(2,1)}, bf16[2,64,896]{2,1,0:T(8,128)(2,1)S(1)}, u32[]{:S(2)}, u32[]{:S(2)}) collective-permute-start(bf16[2,64,896]{2,1,0:T(8,128)(2,1)} %get-tuple-element.47), channel_id=1, source_target_pairs={{0,20},{4,16},{8,28},{12,24},{16,4},{20,0},{24,12},{28,8},{1,21},{... | collective-permute-start | bytes 688136 | tf_op jit(solution)/shard_map/ppermute | solution.py:32
  30.1 3.0 %collective-permute-done.19.refs_4_ = bf16[2,64,896]{2,1,0:T(8,128)(2,1)S(1)} collective-permute-done((bf16[2,64,896]{2,1,0:T(8,128)(2,1)}, bf16[2,64,896]{2,1,0:T(8,128)(2,1)S(1)}, u32[]{:S(2)}, u32[]{:S(2)}) %collective-permute-start.19) | collective-permute-done | bytes 229408 | tf_op jit(solution)/shard_map/ppermute | solution.py:32
  33.1 3.5 %collective-permute-start.13 = (bf16[2,64,896]{2,1,0:T(8,128)(2,1)}, bf16[2,64,896]{2,1,0:T(8,128)(2,1)S(1)}, u32[]{:S(2)}, u32[]{:S(2)}) collective-permute-start(bf16[2,64,896]{2,1,0:T(8,128)(2,1)} %get-tuple-element.48), channel_id=1, source_target_pairs={{0,24},{4,28},{8,16},{12,20},{16,8},{20,12},{24,0},{28,4},{1,25},{... | collective-permute-start | bytes 688136 | tf_op jit(solution)/shard_map/ppermute | solution.py:32
  36.6 5.5 %collective-permute-start.15 = (bf16[2,64,896]{2,1,0:T(8,128)(2,1)}, bf16[2,64,896]{2,1,0:T(8,128)(2,1)}, u32[]{:S(2)}, u32[]{:S(2)}) collective-permute-start(bf16[2,64,896]{2,1,0:T(8,128)(2,1)} %get-tuple-element.49), channel_id=1, source_target_pairs={{0,28},{4,24},{8,20},{12,16},{16,12},{20,8},{24,4},{28,0},{1,29},{... | collective-permute-start | bytes 688136 | tf_op jit(solution)/shard_map/ppermute | solution.py:32
  42.1 8.9 %collective-permute-done.9.refs_0_ = bf16[2,64,896]{2,1,0:T(8,128)(2,1)S(1)} collective-permute-done((bf16[2,64,896]{2,1,0:T(8,128)(2,1)}, bf16[2,64,896]{2,1,0:T(8,128)(2,1)S(1)}, u32[]{:S(2)}, u32[]{:S(2)}) %collective-permute-start.9) | collective-permute-done | bytes 229408 | tf_op jit(solution)/shard_map/ppermute | solution.py:32
  51.0 3.4 %abs_reduce_fusion = bf16[]{:T(256)} fusion(bf16[4096,512]{1,0:T(8,128)(2,1)} %param.12), kind=kLoop, calls=%fused_computation.2 | loop fusion | flops 4194303 | bytes 4194306 | tf_op jit(solution)/shard_map/reduce_max | solution.py:441
  57.6 3.2 %fusion.18 = f32[512,512]{1,0:T(8,128)} fusion(bf16[512,1024]{1,0:T(8,128)(2,1)} %param.9, bf16[4096,512]{1,0:T(8,128)(2,1)} %param.12, s32[]{:T(128)S(6)} %select_n.21), kind=kOutput, calls=%fused_computation.33 | convolution fusion | flops 536870912 | bytes 3145732 | tf_op jit(solution)/shard_map/dot_general | solution.py:463
  64.7 3.3 %fusion.13 = f32[512,512]{1,0:T(8,128)} fusion(bf16[512,1024]{1,0:T(8,128)(2,1)} %param.10, bf16[512,4096]{1,0:T(8,128)(2,1)} %param.15, s32[]{:T(128)S(6)} %select_n.21), kind=kOutput, calls=%fused_computation.28 | convolution fusion | flops 536870912 | bytes 3145732 | tf_op jit(solution)/shard_map/dot_general | solution.py:468
  74.3 5.7 %project.2 = (bf16[2048,512]{1,0:T(8,128)(2,1)}, bf16[2048,512]{1,0:T(8,128)(2,1)}) custom-call(s32[2]{0:T(128)} %pad_add_fusion.3.place_ref, bf16[2,64,896]{2,1,0:T(8,128)(2,1)} %get-tuple-element.50.refs_0_, bf16[2,64,896]{2,1,0:T(8,128)(2,1)} %get-tuple-element.51.refs_1_, bf16[2,64,896]{2,1,0:T(8,128)(2,1)} %copy-done.25, ...), custom_call_target="tpu_custom_call" | custom-call | flops 1879048192 | bytes 3932160 | tf_op jit(solution)/shard_map/project/pallas_call | solution.py:172
  80.5 5.4 %project.3 = (bf16[2048,512]{1,0:T(8,128)(2,1)}, bf16[2048,512]{1,0:T(8,128)(2,1)}) custom-call(s32[2]{0:T(128)} %pad_add_fusion.3.place_ref, bf16[2,64,896]{2,1,0:T(8,128)(2,1)} %copy-done.17, bf16[2,64,896]{2,1,0:T(8,128)(2,1)} %copy-done.20, bf16[2,64,896]{2,1,0:T(8,128)(2,1)} %copy-done.18, ...), custom_call_target="tpu_custom_call", output_to_operand_aliasing={{0}: (11, {}), {1}: (12, {})} | custom-call | flops 1879048192 | bytes 3932160 | tf_op jit(solution)/shard_map/project/pallas_call | solution.py:172
  85.9 3.0 %collective-permute-done.7 = bf16[512,1024]{1,0:T(8,128)(2,1)} collective-permute-done((bf16[512,1024]{1,0:T(8,128)(2,1)}, bf16[512,1024]{1,0:T(8,128)(2,1)}, u32[]{:S(2)}, u32[]{:S(2)}) %collective-permute-start.7) | collective-permute-done | bytes 1048608 | tf_op jit(solution)/shard_map/ppermute | solution.py:32
  88.9 21.6 %collective-permute-done.4 = bf16[512,1024]{1,0:T(8,128)(2,1)} collective-permute-done((bf16[512,1024]{1,0:T(8,128)(2,1)}, bf16[512,1024]{1,0:T(8,128)(2,1)}, u32[]{:S(2)}, u32[]{:S(2)}) %collective-permute-start.4) | collective-permute-done | bytes 1048608 | tf_op jit(solution)/shard_map/ppermute | solution.py:32
  122.5 9.8 %attend.1 = (bf16[2,128,512]{2,1,0:T(8,128)(2,1)S(1)}, bf16[2,128,512]{2,1,0:T(8,128)(2,1)S(1)}, f32[8,128]{1,0:T(8,128)S(1)}, bf16[512,1024]{1,0:T(8,128)(2,1)S...) custom-call(s32[2]{0:T(128)S(1)} %copy-done.2, s32[48]{0:T(128)S(1)} %copy-done.3, ...), custom_call_target="tpu_custom_call" | custom-call | flops 6442450944 | bytes 10485760 | tf_op jit(solution)/shard_map/attend/pallas_call | solution.py:338
  141.9 3.6 %convolution_convert_fusion = bf16[256,4096]{1,0:T(8,128)(2,1)S(1)} fusion(bf16[256,512]{1,0:T(8,128)(2,1)S(1)} %bitcast.66, bf16[4096,512]{1,0:T(8,128)(2,1)} %collective-permute-done.23.ready_query), kind=kOutput, calls=%fused_computation | convolution fusion | flops 1074790400 | bytes 6553600 | tf_op jit(solution)/shard_map/dot_general | solution.py:522
  162.4 5.5 %collective-permute-start.37 = (f32[2,128]{1,0:T(2,128)S(1)}, f32[2,128]{1,0:T(2,128)S(1)}, u32[]{:S(2)}, u32[]{:S(2)}) collective-permute-start(f32[2,128]{1,0:T(2,128)S(1)} %pad_maximum_fusion.1), channel_id=1, source_target_pairs={{0,8},{4,12},{8,0},{12,4},{16,24},{20,28},{24,16},{28,20},{1,9},{5... | collective-permute-start | bytes 3080 | tf_op jit(solution)/shard_map/ppermute | solution.py:32
  169.8 3.8 %collective-permute-start.40 = (f32[4,128]{1,0:T(4,128)S(1)}, f32[4,128]{1,0:T(4,128)S(1)}, u32[]{:S(2)}, u32[]{:S(2)}) collective-permute-start(f32[4,128]{1,0:T(4,128)S(1)} %pad_maximum_fusion), channel_id=1, source_target_pairs={{0,16},{4,20},{8,24},{12,28},{16,0},{20,4},{24,8},{28,12},{1,17},{... | collective-permute-start | bytes 6152 | tf_op jit(solution)/shard_map/ppermute | solution.py:32
  178.8 2.9 %collective-permute-start.43 = (f16[448,128]{1,0:T(8,128)(2,1)S(1)}, f16[448,128]{1,0:T(8,128)(2,1)S(1)}, u32[]{:S(2)}, u32[]{:S(2)}) collective-permute-start(f16[448,128]{1,0:T(8,128)(2,1)S(1)} %get-tuple-element.80), channel_id=1, source_target_pairs={{0,28},{4,24},{8,20},{12,16},{16,12},{20,8},{24,4},{28,0},{1,29},{... | collective-permute-start | bytes 344072 | tf_op jit(solution)/shard_map/ppermute | solution.py:32
  190.2 4.3 %collective-permute-start.38 = (f16[448,128]{1,0:T(8,128)(2,1)S(1)}, f16[448,128]{1,0:T(8,128)(2,1)S(1)}, u32[]{:S(2)}, u32[]{:S(2)}) collective-permute-start(f16[448,128]{1,0:T(8,128)(2,1)S(1)} %get-tuple-element.76), channel_id=1, source_target_pairs={{0,12},{4,8},{8,4},{12,0},{16,28},{20,24},{24,20},{28,16},{1,13},{... | collective-permute-start | bytes 344072 | tf_op jit(solution)/shard_map/ppermute | solution.py:32
  204.3 3.0 %collect.1 = (f32[224,512]{1,0:T(8,128)}, f32[224,512]{1,0:T(8,128)}) custom-call(s32[8]{0:T(128)} %get-tuple-element.39.asked_ref, s32[2]{0:T(128)} %pad_add_fusion.3.place_ref, f32[448,128]{1,0:T(8,128)} %get-tuple-element.79.refs_0_, f32[448,128]{1,0:T(8,128)} %convert_multiply_fusion.6.refs_1_, f32[448,128]{1,0:T(8,128)} %convert_multiply_fusion.5.refs_2_, ...), custom_call_target="tpu_custom_call" | custom-call | flops 917504 | bytes 1835008 | tf_op jit(solution)/shard_map/collect/pallas_call | solution.py:380
  211.3 2.7 %add_convert_fusion = bf16[128,4096]{1,0:T(8,128)(2,1)} fusion(f16[128,4096]{1,0:T(8,128)(2,1)S(1)} %collective-permute-done.31, f32[]{:T(128)} %bitcast.15, bf16[256,4096]{1,0:T(8,128)(2,1)S(1)} %copy-done.12, s32[]{:T(128)S(6)} %select_n.47, bf16[256,4096]{1,0:T(8,128)(2,1)} %copy-done.13), kind=kLoop, calls=%fused_computation.3 | loop fusion | flops 3670016 | bytes 4194312 | tf_op jit(solution)/shard_map/convert_element_type | solution.py:561
  (182 shorter events, 88.4 us)
Async XLA Ops:
  4.5 116.6 %collective-permute-start.23 = (bf16[4096,512]{1,0:T(8,128)(2,1)}, bf16[4096,512]{1,0:T(8,128)(2,1)}, u32[]{:S(2)}, u32[]{:S(2)}) collective-permute-start(bf16[4096,512]{1,0:T(8,128)(2,1)} %param.12), channel_id=1, source_target_pairs={{0,1},{1,0},{2,3},{3,2},{4,5},{5,4},{6,7},{7,6},{8,9},{9,8},{10,11... | collective-permute-start | bytes 12582920 | tf_op jit(solution)/shard_map/ppermute | solution.py:32
  20.3 12.8 %collective-permute-start.19 = (bf16[2,64,896]{2,1,0:T(8,128)(2,1)}, bf16[2,64,896]{2,1,0:T(8,128)(2,1)S(1)}, u32[]{:S(2)}, u32[]{:S(2)}) collective-permute-start(bf16[2,64,896]{2,1,0:T(8,128)(2,1)} %get-tuple-element.53), channel_id=1, source_target_pairs={{0,8},{4,12},{8,0},{12,4},{16,24},{20,28},{24,16},{28,20},{1,9},{5... | collective-permute-start | bytes 688136 | tf_op jit(solution)/shard_map/ppermute | solution.py:32
  21.9 14.7 %collective-permute-start.21 = (bf16[2,64,896]{2,1,0:T(8,128)(2,1)}, bf16[2,64,896]{2,1,0:T(8,128)(2,1)}, u32[]{:S(2)}, u32[]{:S(2)}) collective-permute-start(bf16[2,64,896]{2,1,0:T(8,128)(2,1)} %get-tuple-element.54), channel_id=1, source_target_pairs={{0,12},{4,8},{8,4},{12,0},{16,28},{20,24},{24,20},{28,16},{1,13},{... | collective-permute-start | bytes 688136 | tf_op jit(solution)/shard_map/ppermute | solution.py:32
  22.0 29.0 %collective-permute-start.9 = (bf16[2,64,896]{2,1,0:T(8,128)(2,1)}, bf16[2,64,896]{2,1,0:T(8,128)(2,1)S(1)}, u32[]{:S(2)}, u32[]{:S(2)}) collective-permute-start(bf16[2,64,896]{2,1,0:T(8,128)(2,1)} %get-tuple-element.46), channel_id=1, source_target_pairs={{0,16},{4,20},{8,24},{12,28},{16,0},{20,4},{24,8},{28,12},{1,17},{... | collective-permute-start | bytes 688136 | tf_op jit(solution)/shard_map/ppermute | solution.py:32
  26.4 30.2 %collective-permute-start.11 = (bf16[2,64,896]{2,1,0:T(8,128)(2,1)}, bf16[2,64,896]{2,1,0:T(8,128)(2,1)S(1)}, u32[]{:S(2)}, u32[]{:S(2)}) collective-permute-start(bf16[2,64,896]{2,1,0:T(8,128)(2,1)} %get-tuple-element.47), channel_id=1, source_target_pairs={{0,20},{4,16},{8,28},{12,24},{16,4},{20,0},{24,12},{28,8},{1,21},{... | collective-permute-start | bytes 688136 | tf_op jit(solution)/shard_map/ppermute | solution.py:32
  33.1 23.5 %collective-permute-start.13 = (bf16[2,64,896]{2,1,0:T(8,128)(2,1)}, bf16[2,64,896]{2,1,0:T(8,128)(2,1)S(1)}, u32[]{:S(2)}, u32[]{:S(2)}) collective-permute-start(bf16[2,64,896]{2,1,0:T(8,128)(2,1)} %get-tuple-element.48), channel_id=1, source_target_pairs={{0,24},{4,28},{8,16},{12,20},{16,8},{20,12},{24,0},{28,4},{1,25},{... | collective-permute-start | bytes 688136 | tf_op jit(solution)/shard_map/ppermute | solution.py:32
  36.6 20.5 %collective-permute-start.15 = (bf16[2,64,896]{2,1,0:T(8,128)(2,1)}, bf16[2,64,896]{2,1,0:T(8,128)(2,1)}, u32[]{:S(2)}, u32[]{:S(2)}) collective-permute-start(bf16[2,64,896]{2,1,0:T(8,128)(2,1)} %get-tuple-element.49), channel_id=1, source_target_pairs={{0,28},{4,24},{8,20},{12,16},{16,12},{20,8},{24,4},{28,0},{1,29},{... | collective-permute-start | bytes 688136 | tf_op jit(solution)/shard_map/ppermute | solution.py:32
  60.8 19.1 %collective-permute-start.6 = (bf16[512,1024]{1,0:T(8,128)(2,1)}, bf16[512,1024]{1,0:T(8,128)(2,1)S(1)}, u32[]{:S(2)}, u32[]{:S(2)}) collective-permute-start(bf16[512,1024]{1,0:T(8,128)(2,1)} %param.10), channel_id=1, source_target_pairs={{0,1},{1,0},{2,3},{3,2},{4,5},{5,4},{6,7},{7,6},{8,9},{9,8},{10,11... | collective-permute-start | bytes 3145736 | tf_op jit(solution)/shard_map/ppermute | solution.py:32
  62.5 26.3 %collective-permute-start.7 = (bf16[512,1024]{1,0:T(8,128)(2,1)}, bf16[512,1024]{1,0:T(8,128)(2,1)}, u32[]{:S(2)}, u32[]{:S(2)}) collective-permute-start(bf16[512,1024]{1,0:T(8,128)(2,1)} %param.10), channel_id=1, source_target_pairs={{0,2},{1,3},{2,0},{3,1},{4,6},{5,7},{6,4},{7,5},{8,10},{9,11},{10,... | collective-permute-start | bytes 3145736 | tf_op jit(solution)/shard_map/ppermute | solution.py:32
  64.0 46.4 %collective-permute-start.4 = (bf16[512,1024]{1,0:T(8,128)(2,1)}, bf16[512,1024]{1,0:T(8,128)(2,1)}, u32[]{:S(2)}, u32[]{:S(2)}) collective-permute-start(bf16[512,1024]{1,0:T(8,128)(2,1)} %param.9), channel_id=1, source_target_pairs={{0,2},{1,3},{2,0},{3,1},{4,6},{5,7},{6,4},{7,5},{8,10},{9,11},{10,... | collective-permute-start | bytes 3145736 | tf_op jit(solution)/shard_map/ppermute | solution.py:32
  72.2 42.7 %collective-permute-start.3 = (bf16[512,1024]{1,0:T(8,128)(2,1)}, bf16[512,1024]{1,0:T(8,128)(2,1)}, u32[]{:S(2)}, u32[]{:S(2)}) collective-permute-start(bf16[512,1024]{1,0:T(8,128)(2,1)} %param.9), channel_id=1, source_target_pairs={{0,1},{1,0},{2,3},{3,2},{4,5},{5,4},{6,7},{7,6},{8,9},{9,8},{10,11... | collective-permute-start | bytes 3145736 | tf_op jit(solution)/shard_map/ppermute | solution.py:32
  79.9 41.1 %collective-permute-start.24 = (bf16[896,1024]{1,0:T(8,128)(2,1)}, bf16[896,1024]{1,0:T(8,128)(2,1)S(1)}, u32[]{:S(2)}, u32[]{:S(2)}) collective-permute-start(bf16[896,1024]{1,0:T(8,128)(2,1)} %constant_dynamic-update-slice_fusion), channel_id=1, source_target_pairs={{0,1},{1,0},{2,3},{3,2},{4,5},{5,4},{6,7},{7,6},{8,9},{9,8},{10,11... | collective-permute-start | bytes 5505032 | tf_op jit(solution)/shard_map/ppermute | solution.py:32
  88.9 30.6 %collective-permute-start.8 = (bf16[512,1024]{1,0:T(8,128)(2,1)}, bf16[512,1024]{1,0:T(8,128)(2,1)S(1)}, u32[]{:S(2)}, u32[]{:S(2)}) collective-permute-start(bf16[512,1024]{1,0:T(8,128)(2,1)} %collective-permute-done.7), channel_id=1, source_target_pairs={{0,1},{1,0},{2,3},{3,2},{4,5},{5,4},{6,7},{7,6},{8,9},{9,8},{10,11... | collective-permute-start | bytes 3145736 | tf_op jit(solution)/shard_map/ppermute | solution.py:32
  110.5 9.8 %collective-permute-start.5 = (bf16[512,1024]{1,0:T(8,128)(2,1)}, bf16[512,1024]{1,0:T(8,128)(2,1)S(1)}, u32[]{:S(2)}, u32[]{:S(2)}) collective-permute-start(bf16[512,1024]{1,0:T(8,128)(2,1)} %collective-permute-done.4), channel_id=1, source_target_pairs={{0,1},{1,0},{2,3},{3,2},{4,5},{5,4},{6,7},{7,6},{8,9},{9,8},{10,11... | collective-permute-start | bytes 3145736 | tf_op jit(solution)/shard_map/ppermute | solution.py:32
  134.3 11.2 %collective-permute-start.25 = (bf16[512,1024]{1,0:T(8,128)(2,1)}, bf16[512,1024]{1,0:T(8,128)(2,1)}, u32[]{:S(2)}, u32[]{:S(2)}) collective-permute-start(bf16[512,1024]{1,0:T(8,128)(2,1)} %get-tuple-element.62), channel_id=1, source_target_pairs={{0,1},{1,0},{2,3},{3,2},{4,5},{5,4},{6,7},{7,6},{8,9},{9,8},{10,11... | collective-permute-start | bytes 3145736 | tf_op jit(solution)/shard_map/ppermute | solution.py:32
  136.7 16.2 %collective-permute-start.29 = (bf16[512,1024]{1,0:T(8,128)(2,1)S(1)}, bf16[512,1024]{1,0:T(8,128)(2,1)S(1)}, u32[]{:S(2)}, u32[]{:S(2)}) collective-permute-start(bf16[512,1024]{1,0:T(8,128)(2,1)S(1)} %get-tuple-element.66), channel_id=1, source_target_pairs={{0,1},{1,0},{2,3},{3,2},{4,5},{5,4},{6,7},{7,6},{8,9},{9,8},{10,11... | collective-permute-start | bytes 3145736 | tf_op jit(solution)/shard_map/ppermute | solution.py:32
  150.2 28.4 %collective-permute-start.32 = (f16[448,512]{1,0:T(8,128)(2,1)S(1)}, f16[448,512]{1,0:T(8,128)(2,1)S(1)}, u32[]{:S(2)}, u32[]{:S(2)}) collective-permute-start(f16[448,512]{1,0:T(8,128)(2,1)S(1)} %fusion.8), channel_id=1, source_target_pairs={{0,2},{1,3},{2,0},{3,1},{4,6},{5,7},{6,4},{7,5},{8,10},{9,11},{10,... | collective-permute-start | bytes 1376264 | tf_op jit(solution)/shard_map/ppermute | solution.py:32
  153.7 33.4 %collective-permute-start.33 = (f16[448,512]{1,0:T(8,128)(2,1)S(1)}, f16[448,512]{1,0:T(8,128)(2,1)S(1)}, u32[]{:S(2)}, u32[]{:S(2)}) collective-permute-start(f16[448,512]{1,0:T(8,128)(2,1)S(1)} %fusion.9), channel_id=1, source_target_pairs={{0,2},{1,3},{2,0},{3,1},{4,6},{5,7},{6,4},{7,5},{8,10},{9,11},{10,... | collective-permute-start | bytes 1376264 | tf_op jit(solution)/shard_map/ppermute | solution.py:32
  158.2 53.1 %collective-permute-start.31 = (f16[128,4096]{1,0:T(8,128)(2,1)}, f16[128,4096]{1,0:T(8,128)(2,1)S(1)}, u32[]{:S(2)}, u32[]{:S(2)}) collective-permute-start(f16[128,4096]{1,0:T(8,128)(2,1)} %multiply_convert_fusion), channel_id=1, source_target_pairs={{0,2},{1,3},{2,0},{3,1},{4,6},{5,7},{6,4},{7,5},{8,10},{9,11},{10,... | collective-permute-start | bytes 3145736 | tf_op jit(solution)/shard_map/ppermute | solution.py:32
  178.8 11.3 %collective-permute-start.43 = (f16[448,128]{1,0:T(8,128)(2,1)S(1)}, f16[448,128]{1,0:T(8,128)(2,1)S(1)}, u32[]{:S(2)}, u32[]{:S(2)}) collective-permute-start(f16[448,128]{1,0:T(8,128)(2,1)S(1)} %get-tuple-element.80), channel_id=1, source_target_pairs={{0,28},{4,24},{8,20},{12,16},{16,12},{20,8},{24,4},{28,0},{1,29},{... | collective-permute-start | bytes 344072 | tf_op jit(solution)/shard_map/ppermute | solution.py:32
  181.7 13.4 %collective-permute-start.42 = (f16[448,128]{1,0:T(8,128)(2,1)S(1)}, f16[448,128]{1,0:T(8,128)(2,1)S(1)}, u32[]{:S(2)}, u32[]{:S(2)}) collective-permute-start(f16[448,128]{1,0:T(8,128)(2,1)S(1)} %get-tuple-element.81), channel_id=1, source_target_pairs={{0,24},{4,28},{8,16},{12,20},{16,8},{20,12},{24,0},{28,4},{1,25},{... | collective-permute-start | bytes 344072 | tf_op jit(solution)/shard_map/ppermute | solution.py:32
  183.1 15.7 %collective-permute-start.41 = (f16[448,128]{1,0:T(8,128)(2,1)S(1)}, f16[448,128]{1,0:T(8,128)(2,1)S(1)}, u32[]{:S(2)}, u32[]{:S(2)}) collective-permute-start(f16[448,128]{1,0:T(8,128)(2,1)S(1)} %get-tuple-element.82), channel_id=1, source_target_pairs={{0,20},{4,16},{8,28},{12,24},{16,4},{20,0},{24,12},{28,8},{1,21},{... | collective-permute-start | bytes 344072 | tf_op jit(solution)/shard_map/ppermute | solution.py:32
  187.1 13.4 %collective-permute-start.39 = (f16[448,128]{1,0:T(8,128)(2,1)S(1)}, f16[448,128]{1,0:T(8,128)(2,1)S(1)}, u32[]{:S(2)}, u32[]{:S(2)}) collective-permute-start(f16[448,128]{1,0:T(8,128)(2,1)S(1)} %get-tuple-element.83), channel_id=1, source_target_pairs={{0,16},{4,20},{8,24},{12,28},{16,0},{20,4},{24,8},{28,12},{1,17},{... | collective-permute-start | bytes 344072 | tf_op jit(solution)/shard_map/ppermute | solution.py:32
  190.2 11.1 %collective-permute-start.38 = (f16[448,128]{1,0:T(8,128)(2,1)S(1)}, f16[448,128]{1,0:T(8,128)(2,1)S(1)}, u32[]{:S(2)}, u32[]{:S(2)}) collective-permute-start(f16[448,128]{1,0:T(8,128)(2,1)S(1)} %get-tuple-element.76), channel_id=1, source_target_pairs={{0,12},{4,8},{8,4},{12,0},{16,28},{20,24},{24,20},{28,16},{1,13},{... | collective-permute-start | bytes 344072 | tf_op jit(solution)/shard_map/ppermute | solution.py:32
  (51 other events, 353.9 us)
